TPU v7x, 32 devices: a whole 2x2x4 slice. The times are simulated.
32 devices in a mesh: batch: 4 (over x, core), cache: 8 (over z, y).
Axes of the slice: x: 2, y: 2, z: 4, core: 2. Of those that a mesh axis runs over, the one named last changes fastest.
Arguments:
- arrivals: bfloat16 [16, 4, 4096], P('batch', None, 'cache'), may hold values from -6 to 6
- norm_gain: float32 [4096], replicated, may hold values from 0.25 to 1.75
- qkv_weight: bfloat16 [4096, 6144], P(None, 'cache'), may hold values from -0.09375 to 0.09375
- out_weight: bfloat16 [4096, 4096], P('cache'), may hold values from -0.09375 to 0.09375
- kv_cache: bfloat16 [16, 16, 2, 8, 128, 128], P('batch', 'cache'), as said below
- slot: int32 [16], replicated, may hold values from 0 to 15, each once
- positions: int32 [16], P('batch'), may hold values from 1664 to 2044
- tile_lists: int32 [16, 8], P('batch'), may hold values from 0 to 15, as said below
Outputs:
- attended: bfloat16 [16, 4, 4096], P('batch', None, 'cache')
Inputs may be any that keep to these rules, and one draw needn't show every extreme that they name: `tile_lists`: tiles of a row are distinct; the first is the tile of position positions - 1, the others lie at most 12 tiles before it. `kv_cache`: entries are of magnitude at most 240.
All inputs are finite; a program needn't handle non-finite values.
Results may differ from a plain program's by a relative error of at most 0.022.
Values may be sent and summed in bfloat16 or wider, within the bound.
A program may use at most 64 MiB of HBM per device.

v0:
```python
import math
import jax
import jax.numpy as jnp
from jax import lax
from jax.sharding import PartitionSpec as P

HEADS = 32
KVH = 8
HD = 128
TILE = 128
IMW = 64
CW = 16
epsilon = 1e-05
very_low = -1e30


def window_mask(query_pos, key_pos):
    return jnp.abs(key_pos % IMW - query_pos % IMW) <= CW


def shards(arrivals, norm_gain, qkv_weight, out_weight, kv_cache, slot, positions, tile_lists):
    row_count = positions.shape[0]
    step_count = arrivals.shape[1]
    groups = HEADS // KVH
    head_share = out_weight.shape[0] // HD
    head_start = lax.axis_index("cache") * head_share
    everyone = lax.all_gather(arrivals, "batch", axis=0, tiled=True)
    inverse = jnp.argsort(slot)
    my_rows = lax.dynamic_slice_in_dim(inverse, lax.axis_index("batch") * row_count, row_count)
    picked = jnp.take(everyone, my_rows, axis=0)
    whole = lax.all_gather(picked, "cache", axis=2, tiled=True)
    wide_values = whole.astype(jnp.float32)
    normed = (
        wide_values
        * lax.rsqrt(jnp.mean(wide_values * wide_values, axis=-1, keepdims=True) + epsilon)
        * norm_gain
    ).astype(jnp.bfloat16)
    projected = jnp.dot(
        normed.reshape(row_count * step_count, -1), qkv_weight, preferred_element_type=jnp.float32
    )
    projected = projected.astype(jnp.bfloat16).reshape(row_count, step_count, -1)
    heads_all = lax.all_gather(projected, "cache", axis=2, tiled=True).reshape(
        row_count, step_count, KVH, groups + 2, HD
    )
    queries = heads_all[:, :, :, :groups, :]
    new_keys = heads_all[:, :, :, groups, :]
    new_vals = heads_all[:, :, :, groups + 1, :]
    score_scale = 1.0 / math.sqrt(HD)
    tiles_here = kv_cache.shape[1]
    tile_ids = lax.axis_index("cache") * tiles_here + jnp.arange(tiles_here, dtype=jnp.int32)
    listed = jnp.any(tile_lists[:, :, None] == tile_ids[None, None, :], axis=1)
    key_pos = tile_ids[:, None] * TILE + jnp.arange(TILE, dtype=jnp.int32)[None, :]
    step_index = jnp.arange(step_count, dtype=jnp.int32)
    query_pos = positions[:, None] + step_index[None, :]
    key_valid = listed[:, None, :, None] & (key_pos[None, None] < positions[:, None, None, None])
    key_valid = key_valid & window_mask(query_pos[:, :, None, None], key_pos[None, None])
    valid_wide = key_valid[:, None, None]
    scores = (
        jnp.einsum(
            "bsjgd,btjkd->bjgstk", queries, kv_cache[:, :, 0], preferred_element_type=jnp.float32
        )
        * score_scale
    )
    new_valid = (step_index[None, :, None] >= step_index[None, None, :]) & window_mask(
        query_pos[:, :, None], query_pos[:, None, :]
    )
    new_scores = (
        jnp.einsum("bsjgd,bujd->bjgsu", queries, new_keys, preferred_element_type=jnp.float32)
        * score_scale
    )
    new_max = jnp.max(jnp.where(new_valid[:, None, None], new_scores, -jnp.inf), axis=-1)
    local_max = jnp.max(jnp.where(valid_wide, scores, very_low), axis=(-2, -1))
    values_here = kv_cache[:, :, 1]

    def own_heads(array):
        merged = array.reshape((row_count, HEADS) + array.shape[3:])
        return lax.dynamic_slice_in_dim(merged, head_start, head_share, 1)

    weights = jnp.where(valid_wide, jnp.exp(scores - local_max[..., None, None]), 0.0)
    totals = jnp.sum(weights, axis=(-2, -1))
    numerator = jnp.einsum(
        "bjgstk,btjkd->bjgsd",
        weights.astype(jnp.bfloat16),
        values_here,
        preferred_element_type=jnp.float32,
    )
    part_sums, part_totals, part_peaks = (
        lax.all_to_all(
            numerator.reshape(1, row_count, HEADS, step_count, HD).astype(jnp.bfloat16),
            "cache",
            split_axis=2,
            concat_axis=0,
            tiled=True,
        ).astype(jnp.float32),
        lax.all_to_all(
            totals.reshape(1, row_count, HEADS, step_count).astype(jnp.bfloat16),
            "cache",
            split_axis=2,
            concat_axis=0,
            tiled=True,
        ).astype(jnp.float32),
        lax.all_to_all(
            local_max.reshape(1, row_count, HEADS, step_count).astype(jnp.bfloat16),
            "cache",
            split_axis=2,
            concat_axis=0,
            tiled=True,
        ).astype(jnp.float32),
    )
    top_own = jnp.maximum(jnp.max(part_peaks, axis=0), own_heads(new_max))
    factor = jnp.exp(part_peaks - top_own[None])
    numer_own = jnp.sum(part_sums * factor[..., None], axis=0)
    total_own = jnp.sum(part_totals * factor, axis=0)
    own_new = own_heads(new_scores)
    new_weights = jnp.where(new_valid[:, None], jnp.exp(own_new - top_own[..., None]), 0.0)
    own_vals = lax.dynamic_slice_in_dim(
        jnp.repeat(new_vals, groups, axis=2), head_start, head_share, 2
    )
    total_all = total_own + jnp.sum(new_weights, axis=-1)
    numer_all = numer_own + jnp.einsum(
        "bhsu,buhd->bhsd",
        new_weights.astype(jnp.bfloat16),
        own_vals,
        preferred_element_type=jnp.float32,
    )
    attention = (numer_all / total_all[..., None]).astype(jnp.bfloat16)
    attn_flat = attention.transpose(0, 2, 1, 3).reshape(row_count * step_count, head_share * HD)
    partial_out = jnp.dot(attn_flat, out_weight, preferred_element_type=jnp.float32).reshape(
        row_count, step_count, -1
    )
    return lax.psum_scatter(
        partial_out.astype(jnp.bfloat16), "cache", scatter_dimension=2, tiled=True
    )


def solution(mesh):
    in_specs = (
        P("batch", None, "cache"),
        P(),
        P(None, "cache"),
        P("cache", None),
        P("batch", "cache", None, None, None, None),
        P(),
        P("batch"),
        P("batch", None),
    )
    out_specs = P("batch", None, "cache")
    return jax.shard_map(shards, mesh=mesh, in_specs=in_specs, out_specs=out_specs, check_vma=False)
```

profile of v0, /device:TPU:0, one launch (start us, length us, event | category | flops | bytes accessed | tf_op | source)
XLA Modules:
  0.0 208.3 jit_solution(18391242171131757612)
XLA Ops:
  6.5 0.9 compare_reduce_fusion
  8.4 1.9 sort.17
  10.3 6.5 %all_gather.9 = bf16[16,4,512]{2,1,0:T(4,128)(2,1)S(1)} all-gather(bf16[4,4,512]{2,1,0:T(4,128)(2,1)} %param.8), channel_id=1, replica_groups=mesh['batch'=4,'cache'=8] {'batch'}, dimensions={0}, use_global_device_ids=true | all-gather | bytes 81920 | tf_op jit(solution)/shard_map/all_gather | solution.py:27
  17.5 31.3 %all_gather.10 = bf16[4,4,4096]{2,1,0:T(4,128)(2,1)S(1)} all-gather(bf16[4,4,512]{2,1,0:T(4,128)(2,1)S(1)} %broadcast_select_fusion), channel_id=1, replica_groups=mesh['batch'=4,'cache'=8] {'cache'}, dimensions={2}, use_global_device_ids=true | all-gather | bytes 147456 | tf_op jit(solution)/shard_map/all_gather | solution.py:31
  49.0 0.9 fusion.16
  49.9 3.7 %convolution_convert_fusion.1 = bf16[16,768]{1,0:T(8,128)(2,1)S(1)} fusion(bf16[16,4096]{1,0:T(8,128)(2,1)S(1)} %reshape.312, bf16[4096,768]{1,0:T(8,128)(2,1)} %param.10), kind=kOutput, calls=%fused_computation.13 | convolution fusion | flops 100675584 | bytes 6447104 | tf_op jit(solution)/shard_map/dot_general | solution.py:38
  53.6 30.7 %all_gather.11 = bf16[4,4,6144]{2,1,0:T(4,128)(2,1)S(1)} all-gather(bf16[4,4,768]{2,1,0:T(4,128)(2,1)S(1)} %reshape.313), channel_id=1, replica_groups=mesh['batch'=4,'cache'=8] {'cache'}, dimensions={2}, use_global_device_ids=true | all-gather | bytes 221184 | tf_op jit(solution)/shard_map/all_gather | solution.py:42
  84.5 2.6 %fusion.37 = (bf16[4,2,1,8,128,128]{5,4,3,2,1,0:T(8,128)(2,1)S(1)}, bf16[4,2,1,8,128,128]{5,4,3,2,1,0:T(8,128)(2,1)S(1)}) fusion(bf16[4,2,2,8,128,128]{5,4,3,2,1,0:T(8,128)(2,1)} %param.12), kind=kLoop, calls=%fused_computation.74 | loop fusion | bytes 8388608 | tf_op jit(solution)/shard_map/slice | solution.py:73
  87.4 0.8 select_reduce_fusion
  88.3 0.8 copy.116
  89.1 5.5 %all-to-all-start.1 = ((bf16[1,4,32,4]{3,1,0,2:T(4,128)(2,1)}), bf16[1,4,32,4]{3,1,0,2:T(4,128)(2,1)S(1)}, u32[]{:S(2)}, u32[]{:S(2)}) async-start(bf16[1,4,32,4]{3,1,0,2:T(4,128)(2,1)} %bitcast.15), calls=%async_computation.1 | async-start | bytes 65536 | tf_op jit(solution)/shard_map/all_to_all | solution.py:102
  95.7 1.3 select_reduce_fusion.1
  98.3 0.8 copy.120
  99.1 2.2 %all-to-all-done.1 = bf16[1,4,32,4]{3,1,0,2:T(4,128)(2,1)S(1)} async-done(((bf16[1,4,32,4]{3,1,0,2:T(4,128)(2,1)}), bf16[1,4,32,4]{3,1,0,2:T(4,128)(2,1)S(1)}, u32[]{:S(2)}, u32[]{:S(2)}) %all-to-all-start.1) | async-done | bytes 1056 | tf_op jit(solution)/shard_map/all_to_all | solution.py:102
  101.3 3.8 %all-to-all-start.2 = ((bf16[1,4,32,4]{3,1,0,2:T(4,128)(2,1)}), bf16[1,4,32,4]{3,1,0,2:T(4,128)(2,1)S(1)}, u32[]{:S(2)}, u32[]{:S(2)}) async-start(bf16[1,4,32,4]{3,1,0,2:T(4,128)(2,1)} %bitcast.26), calls=%async_computation.2 | async-start | bytes 65536 | tf_op jit(solution)/shard_map/all_to_all | solution.py:95
  105.4 6.3 %all-to-all-done.2 = bf16[1,4,32,4]{3,1,0,2:T(4,128)(2,1)S(1)} async-done(((bf16[1,4,32,4]{3,1,0,2:T(4,128)(2,1)}), bf16[1,4,32,4]{3,1,0,2:T(4,128)(2,1)S(1)}, u32[]{:S(2)}, u32[]{:S(2)}) %all-to-all-start.2) | async-done | bytes 1056 | tf_op jit(solution)/shard_map/all_to_all | solution.py:95
  111.8 3.4 %all-to-all-start = ((bf16[1,4,32,4,128]{4,3,1,0,2:T(4,128)(2,1)}), bf16[1,4,32,4,128]{4,3,1,0,2:T(4,128)(2,1)S(1)}, u32[]{:S(2)}, u32[]{:S(2)}) async-start(bf16[1,4,32,4,128]{4,3,1,0,2:T(4,128)(2,1)} %copy.94), calls=%async_computation | async-start | bytes 262144 | tf_op jit(solution)/shard_map/all_to_all | solution.py:88
  116.3 6.1 %all-to-all-done = bf16[1,4,32,4,128]{4,3,1,0,2:T(4,128)(2,1)S(1)} async-done(((bf16[1,4,32,4,128]{4,3,1,0,2:T(4,128)(2,1)}), bf16[1,4,32,4,128]{4,3,1,0,2:T(4,128)(2,1)S(1)}, u32[]{:S(2)}, u32[]{:S(2)}) %all-to-all-start) | async-done | bytes 131104 | tf_op jit(solution)/shard_map/all_to_all | solution.py:88
  122.7 3.0 %convolution_convert_fusion = bf16[4,4,4096]{2,1,0:T(4,128)(2,1)S(1)} fusion(bf16[512,4096]{1,0:T(8,128)(2,1)} %param.11, bf16[4,4,4,4]{3,2,1,0:T(4,128)(2,1)S(1)} %copy.104, f32[4,4,4,128]{3,2,0,1:T(4,128)S(1)} %fusion.17, f32[4,4,4]{1,2,0:T(4,128)S(1)} %copy.110, bf16[4,4,32,128]{3,1,2,0:T(4,128)(2,1)S(1)} %bitcast.113, s32[]{:T(128)S(6)} %select_n.81), kind=kOutput, calls=%fused_computation.1 | convolution fusion | flops 67264512 | bytes 4399108 | tf_op jit(solution)/shard_map/dot_general | solution.py:128
  125.7 4.8 %copy.121 = bf16[4,4,4096]{1,0,2:T(4,128)(2,1)} copy(bf16[4,4,4096]{2,1,0:T(4,128)(2,1)S(1)} %convolution_convert_fusion) | data formatting | bytes 262144
  130.5 6.1 %reshape.338 = bf16[4096,16]{1,0:T(8,128)(2,1)} reshape(bf16[4096,4,4]{2,1,0:T(4,128)(2,1)} %bitcast.110) | data formatting | bytes 262144
  136.6 62.8 %reduce-scatter.4.cloned.1.call-done = bf16[512,16]{1,0:T(8,128)(2,1)} async-done(((bf16[4096,16]{1,0:T(8,128)(2,1)}), bf16[512,16]{1,0:T(8,128)(2,1)}) %reduce-scatter.4.cloned.1.call-update) | async-done | bytes 16400
  199.3 1.1 reshape.339
  200.5 0.9 copy.122
  (46 shorter events, 6.6 us)
Async XLA Ops:
  84.5 2.6 %copy-start = (s32[4]{0:T(128)S(1)}, s32[4]{0:T(128)}, u32[]{:S(2)}) copy-start(s32[4]{0:T(128)} %param.14) | copy-start | bytes 52
  89.1 12.2 %all-to-all-start.1 = ((bf16[1,4,32,4]{3,1,0,2:T(4,128)(2,1)}), bf16[1,4,32,4]{3,1,0,2:T(4,128)(2,1)S(1)}, u32[]{:S(2)}, u32[]{:S(2)}) async-start(bf16[1,4,32,4]{3,1,0,2:T(4,128)(2,1)} %bitcast.15), calls=%async_computation.1 | async-start | bytes 65536 | tf_op jit(solution)/shard_map/all_to_all | solution.py:102
  101.3 10.5 %all-to-all-start.2 = ((bf16[1,4,32,4]{3,1,0,2:T(4,128)(2,1)}), bf16[1,4,32,4]{3,1,0,2:T(4,128)(2,1)S(1)}, u32[]{:S(2)}, u32[]{:S(2)}) async-start(bf16[1,4,32,4]{3,1,0,2:T(4,128)(2,1)} %bitcast.26), calls=%async_computation.2 | async-start | bytes 65536 | tf_op jit(solution)/shard_map/all_to_all | solution.py:95
  111.8 10.7 %all-to-all-start = ((bf16[1,4,32,4,128]{4,3,1,0,2:T(4,128)(2,1)}), bf16[1,4,32,4,128]{4,3,1,0,2:T(4,128)(2,1)S(1)}, u32[]{:S(2)}, u32[]{:S(2)}) async-start(bf16[1,4,32,4,128]{4,3,1,0,2:T(4,128)(2,1)} %copy.94), calls=%async_computation | async-start | bytes 262144 | tf_op jit(solution)/shard_map/all_to_all | solution.py:88
  115.1 84.2 %reduce-scatter.4.cloned.1.call-start = ((), (), s32[]{:S(2)}) async-start(), calls=%async_computation.4 | async-start | bytes 1179648
Sparse Core Ops, SparseCore 0:
  136.7 62.6 reduce-scatter.3
where the time goes:
time: 209 us; the launch traced here: 208 us
  waiting for transfers between devices  77.5 us (37%)
  blocking collectives  68.5 us (33%)
  local copies, waits for them, and re-layouts  20.8 us (10%)
  between operations  13.6 us (7%)
  starting transfers between devices  12.7 us (6%)
  matrix products  9.2 us (4%)
  other arithmetic  6.06 us (3%)
    unnamed x2, waiting for transfers between devices  62.8 us
    all_gather x1, blocking collectives, shards(): whole = lax.all_gather(picked, 'cache', axis=2, tiled=True)  31.3 us
    all_gather x1, blocking collectives, shards(): lax.all_gather(projected, 'cache', axis=2, tiled=True)  30.7 us
    unnamed x6, local copies, waits for them, and re-layouts  12.9 us
    all_gather x1, blocking collectives, shards(): everyone = lax.all_gather(arrivals, 'batch', axis=0, tiled=True)  6.46 us
    all_to_all x1, waiting for transfers between devices, shards(): lax.all_to_all(totals.reshape(1, row_count, HEADS, step_count).astype(jnp...  6.33 us
    all_to_all x1, waiting for transfers between devices, shards(): lax.all_to_all(numerator.reshape(1, row_count, HEADS, step_count, HD).ast...  6.14 us
    all_to_all x1, starting transfers between devices, shards(): lax.all_to_all(local_max.reshape(1, row_count, HEADS, step_count).astype(...  5.49 us
  transfers between devices with their start and end apart: 4, of which 4 were waited for; matrix products, arithmetic and copies ran while one was open for 3% of the time, Pallas kernels for 0%

commit v1 on v0

--- a/solution.py
+++ b/solution.py
@@ -14,6 +14,28 @@
 very_low = -1e30
 
 
+def connect_islands(vector, in_dim):
+    tall = list(vector.shape[1:])
+    tall[in_dim] *= vector.shape[0]
+    return jnp.moveaxis(vector, 0, in_dim).reshape(tall)
+
+
+def raise_wall(unit, along_axis):
+    n_dev_all = lax.axis_size(along_axis)
+    tile_out = unit[None]
+    for kk in range(n_dev_all.bit_length() - 1):
+        r2 = 1 << kk
+        state_next = range(n_dev_all)
+        w2 = map(lambda i0: (i0, i0 ^ r2), state_next)
+        d_next = list(w2)
+        everything = lax.ppermute(tile_out, axis_name=along_axis, perm=d_next)
+        o_now = jnp.stack([tile_out, everything])
+        long_array = lax.axis_index(along_axis)
+        all_rows = long_array >> kk & 1
+        tile_out = jnp.where(all_rows == 0, o_now, o_now[::-1]).reshape(-1, *unit.shape)
+    return tile_out
+
+
 def window_mask(query_pos, key_pos):
     return jnp.abs(key_pos % IMW - query_pos % IMW) <= CW
 
@@ -28,7 +50,8 @@
     inverse = jnp.argsort(slot)
     my_rows = lax.dynamic_slice_in_dim(inverse, lax.axis_index("batch") * row_count, row_count)
     picked = jnp.take(everyone, my_rows, axis=0)
-    whole = lax.all_gather(picked, "cache", axis=2, tiled=True)
+    a_next = raise_wall(picked, "cache")
+    whole = connect_islands(a_next, 2)
     wide_values = whole.astype(jnp.float32)
     normed = (
         wide_values

time: 209 us -> 192 us (0.919)
  blocking collectives: 68.5 us -> 38.1 us
  waiting for transfers between devices: 77.5 us -> 82.9 us
  starting transfers between devices: 12.7 us -> 17.6 us
    all_gather x1 -> x0, blocking collectives: 31.3 us -> none  [shards(): whole = lax.all_gather(picked, 'cache', axis=2, tiled=True)]
    ppermute x0 -> x3, starting transfers between devices: none -> 6.35 us  [raise_wall(): everything = lax.ppermute(tile_out, axis_name=along_axis, perm=d_next)]
    ppermute x0 -> x3, waiting for transfers between devices: none -> 4.82 us  [raise_wall(): everything = lax.ppermute(tile_out, axis_name=along_axis, perm=d_next)]
    unnamed x6 -> x9, local copies, waits for them, and re-layouts: 12.9 us -> 13.1 us
  transfers between devices with their start and end apart: 4 -> 7, of which waited for: 4 -> 6; matrix products, arithmetic and copies ran while one was open for 3% -> 6% of each run, Pallas kernels for 0% -> 0%
where the time goes in v1:
time: 192 us; the launch traced here: 191 us
  waiting for transfers between devices  82.9 us (43%)
  blocking collectives  38.1 us (20%)
  local copies, waits for them, and re-layouts  22.6 us (12%)
  starting transfers between devices  17.6 us (9%)
  between operations  13.6 us (7%)
  matrix products  10.8 us (6%)
  other arithmetic  5.58 us (3%)
    unnamed x2, waiting for transfers between devices  62.8 us
    all_gather x1, blocking collectives, shards(): lax.all_gather(projected, 'cache', axis=2, tiled=True)  31.6 us
    unnamed x9, local copies, waits for them, and re-layouts  13.1 us
    all_gather x1, blocking collectives, shards(): everyone = lax.all_gather(arrivals, 'batch', axis=0, tiled=True)  6.46 us
    ppermute x3, starting transfers between devices, raise_wall(): everything = lax.ppermute(tile_out, axis_name=along_axis, perm=d_next)  6.35 us
    all_to_all x1, waiting for transfers between devices, shards(): lax.all_to_all(totals.reshape(1, row_count, HEADS, step_count).astype(jnp...  6.27 us
    all_to_all x1, waiting for transfers between devices, shards(): lax.all_to_all(numerator.reshape(1, row_count, HEADS, step_count, HD).ast...  6.14 us
    ppermute x3, waiting for transfers between devices, raise_wall(): everything = lax.ppermute(tile_out, axis_name=along_axis, perm=d_next)  4.82 us
  transfers between devices with their start and end apart: 7, of which 6 were waited for; matrix products, arithmetic and copies ran while one was open for 6% of the time, Pallas kernels for 0%

profile of v1, /device:TPU:0, one launch (start us, length us, event | category | flops | bytes accessed | tf_op | source)
XLA Modules:
  0.0 191.2 jit_solution(15933415007042894785)
XLA Ops:
  6.5 1.9 sort.17
  8.5 6.5 %all_gather.6 = bf16[16,4,512]{2,1,0:T(4,128)(2,1)S(1)} all-gather(bf16[4,4,512]{2,1,0:T(4,128)(2,1)} %param.8), channel_id=1, replica_groups=mesh['batch'=4,'cache'=8] {'batch'}, dimensions={0}, use_global_device_ids=true | all-gather | bytes 81920 | tf_op jit(solution)/shard_map/all_gather | solution.py:49
  15.6 2.1 %collective-permute-start = (bf16[1,4,4,512]{3,2,1,0:T(4,128)(2,1)S(1)}, bf16[1,4,4,512]{3,2,1,0:T(4,128)(2,1)S(1)}, u32[]{:S(2)}, u32[]{:S(2)}) collective-permute-start(bf16[1,4,4,512]{3,2,1,0:T(4,128)(2,1)S(1)} %bitcast_select_fusion), channel_id=1, source_target_pairs={{0,1},{1,0},{2,3},{3,2},{4,5},{5,4},{6,7},{7,6},{8,9},{9,8},{10,11... | collective-permute-start | bytes 49160 | tf_op jit(solution)/shard_map/ppermute | solution.py:31
  19.6 4.0 %fusion.39 = (bf16[4,2,1,8,128,128]{5,4,3,2,1,0:T(8,128)(2,1)S(1)}, bf16[4,2,1,8,128,128]{5,4,3,2,1,0:T(8,128)(2,1)}) fusion(bf16[4,2,2,8,128,128]{5,4,3,2,1,0:T(8,128)(2,1)} %param.12), kind=kLoop, calls=%fused_computation.83 | loop fusion | bytes 8388608 | tf_op jit(solution)/shard_map/slice | solution.py:96
  23.9 1.6 collective-permute-start.1
  25.6 2.3 %collective-permute-done.1 = bf16[2,4,4,512]{3,2,1,0:T(4,128)(2,1)S(1)} collective-permute-done((bf16[2,4,4,512]{3,2,1,0:T(4,128)(2,1)S(1)}, bf16[2,4,4,512]{3,2,1,0:T(4,128)(2,1)S(1)}, u32[]{:S(2)}, u32[]{:S(2)}) %collective-permute-start.1) | collective-permute-done | bytes 32800 | tf_op jit(solution)/shard_map/ppermute | solution.py:31
  28.0 2.7 %collective-permute-start.2 = (bf16[4,4,4,512]{3,2,1,0:T(4,128)(2,1)S(1)}, bf16[4,4,4,512]{3,2,1,0:T(4,128)(2,1)S(1)}, u32[]{:S(2)}, u32[]{:S(2)}) collective-permute-start(bf16[4,4,4,512]{3,2,1,0:T(4,128)(2,1)S(1)} %bitcast.133), channel_id=1, source_target_pairs={{0,4},{1,5},{2,6},{3,7},{4,0},{5,1},{6,2},{7,3},{8,12},{9,13},{10,... | collective-permute-start | bytes 196616 | tf_op jit(solution)/shard_map/ppermute | solution.py:31
  30.7 2.5 %collective-permute-done.2 = bf16[4,4,4,512]{3,2,1,0:T(4,128)(2,1)S(1)} collective-permute-done((bf16[4,4,4,512]{3,2,1,0:T(4,128)(2,1)S(1)}, bf16[4,4,4,512]{3,2,1,0:T(4,128)(2,1)S(1)}, u32[]{:S(2)}, u32[]{:S(2)}) %collective-permute-start.2) | collective-permute-done | bytes 65568 | tf_op jit(solution)/shard_map/ppermute | solution.py:31
  34.0 3.7 %convolution_convert_fusion.1 = bf16[16,768]{1,0:T(8,128)(2,1)S(1)} fusion(bf16[4096,768]{1,0:T(8,128)(2,1)} %param.10, f32[16,4096]{1,0:T(8,128)S(1)} %bitcast.131, f32[4096]{0:T(1024)S(1)} %copy-done, f32[16]{0:T(128)S(1)} %rsqrt.12), kind=kOutput, calls=%fused_computation.13 | convolution fusion | flops 100872192 | bytes 6594624 | tf_op jit(solution)/shard_map/dot_general | solution.py:61
  37.8 31.6 %all_gather.7 = bf16[4,4,6144]{2,1,0:T(4,128)(2,1)S(1)} all-gather(bf16[4,4,768]{2,1,0:T(4,128)(2,1)S(1)} %reshape.349), channel_id=1, replica_groups=mesh['batch'=4,'cache'=8] {'cache'}, dimensions={2}, use_global_device_ids=true | all-gather | bytes 221184 | tf_op jit(solution)/shard_map/all_gather | solution.py:65
  69.7 2.4 %select_reduce_fusion = (f32[4,8,4,4]{2,3,1,0:T(4,128)S(1)}, f32[4,8,4,4,2,128]{5,2,4,3,1,0:T(4,128)S(1)}) fusion(pred[4,4,2,128]{3,2,1,0:T(4,128)(4,1)S(1)} %compare_and_fusion, bf16[4,2,1,8,128,128]{5,4,3,2,1,0:T(8,128)(2,1)} %get-tuple-element.10, bf16[4,4,8,6,128]{4,3,2,1,0:T(8,128)(2,1)S(1)} %reshape.350), kind=kOutput, calls=%fused_computation.20 | convolution fusion | flops 33947136 | bytes 2762752 | tf_op jit(solution)/shard_map/bsjgd,btjkd->bjgstk/dot_general | solution.py:82
  73.5 4.5 %all-to-all-start.1 = ((bf16[1,4,32,4]{3,1,0,2:T(4,128)(2,1)}), bf16[1,4,32,4]{3,1,0,2:T(4,128)(2,1)S(1)}, u32[]{:S(2)}, u32[]{:S(2)}) async-start(bf16[1,4,32,4]{3,1,0,2:T(4,128)(2,1)} %bitcast.26), calls=%async_computation.1 | async-start | bytes 65536 | tf_op jit(solution)/shard_map/all_to_all | solution.py:125
  78.5 1.3 select_reduce_fusion.1
  81.8 2.9 %all-to-all-done.1 = bf16[1,4,32,4]{3,1,0,2:T(4,128)(2,1)S(1)} async-done(((bf16[1,4,32,4]{3,1,0,2:T(4,128)(2,1)}), bf16[1,4,32,4]{3,1,0,2:T(4,128)(2,1)S(1)}, u32[]{:S(2)}, u32[]{:S(2)}) %all-to-all-start.1) | async-done | bytes 1056 | tf_op jit(solution)/shard_map/all_to_all | solution.py:125
  84.7 3.3 %all-to-all-start.2 = ((bf16[1,4,32,4]{3,1,0,2:T(4,128)(2,1)}), bf16[1,4,32,4]{3,1,0,2:T(4,128)(2,1)S(1)}, u32[]{:S(2)}, u32[]{:S(2)}) async-start(bf16[1,4,32,4]{3,1,0,2:T(4,128)(2,1)} %bitcast.37), calls=%async_computation.2 | async-start | bytes 65536 | tf_op jit(solution)/shard_map/all_to_all | solution.py:118
  88.4 6.3 %all-to-all-done.2 = bf16[1,4,32,4]{3,1,0,2:T(4,128)(2,1)S(1)} async-done(((bf16[1,4,32,4]{3,1,0,2:T(4,128)(2,1)}), bf16[1,4,32,4]{3,1,0,2:T(4,128)(2,1)S(1)}, u32[]{:S(2)}, u32[]{:S(2)}) %all-to-all-start.2) | async-done | bytes 1056 | tf_op jit(solution)/shard_map/all_to_all | solution.py:118
  94.7 3.4 %all-to-all-start = ((bf16[1,4,32,4,128]{4,3,1,0,2:T(4,128)(2,1)}), bf16[1,4,32,4,128]{4,3,1,0,2:T(4,128)(2,1)S(1)}, u32[]{:S(2)}, u32[]{:S(2)}) async-start(bf16[1,4,32,4,128]{4,3,1,0,2:T(4,128)(2,1)} %copy.100), calls=%async_computation | async-start | bytes 262144 | tf_op jit(solution)/shard_map/all_to_all | solution.py:111
  99.2 6.1 %all-to-all-done = bf16[1,4,32,4,128]{4,3,1,0,2:T(4,128)(2,1)S(1)} async-done(((bf16[1,4,32,4,128]{4,3,1,0,2:T(4,128)(2,1)}), bf16[1,4,32,4,128]{4,3,1,0,2:T(4,128)(2,1)S(1)}, u32[]{:S(2)}, u32[]{:S(2)}) %all-to-all-start) | async-done | bytes 131104 | tf_op jit(solution)/shard_map/all_to_all | solution.py:111
  105.6 3.0 %convolution_convert_fusion = bf16[4,4,4096]{2,1,0:T(4,128)(2,1)S(1)} fusion(bf16[512,4096]{1,0:T(8,128)(2,1)} %param.11, bf16[4,4,4,4]{3,2,1,0:T(4,128)(2,1)S(1)} %copy.110, f32[4,4,4,128]{3,2,0,1:T(4,128)S(1)} %fusion.14, f32[4,4,4]{1,2,0:T(4,128)S(1)} %copy.116, bf16[4,4,32,128]{3,1,2,0:T(4,128)(2,1)S(1)} %bitcast.135, s32[]{:T(128)S(6)} %select_n.128), kind=kOutput, calls=%fused_computation.1 | convolution fusion | flops 67264512 | bytes 4399108 | tf_op jit(solution)/shard_map/dot_general | solution.py:151
  108.6 4.8 %copy.128 = bf16[4,4,4096]{1,0,2:T(4,128)(2,1)} copy(bf16[4,4,4096]{2,1,0:T(4,128)(2,1)S(1)} %convolution_convert_fusion) | data formatting | bytes 262144
  113.4 6.1 %reshape.376 = bf16[4096,16]{1,0:T(8,128)(2,1)} reshape(bf16[4096,4,4]{2,1,0:T(4,128)(2,1)} %bitcast.127) | data formatting | bytes 262144
  119.5 62.8 %reduce-scatter.4.cloned.1.call-done = bf16[512,16]{1,0:T(8,128)(2,1)} async-done(((bf16[4096,16]{1,0:T(8,128)(2,1)}), bf16[512,16]{1,0:T(8,128)(2,1)}) %reduce-scatter.4.cloned.1.call-update) | async-done | bytes 16400
  182.2 1.1 reshape.377
  183.4 0.9 copy.129
  (61 shorter events, 9.8 us)
Async XLA Ops:
  15.6 8.2 %collective-permute-start = (bf16[1,4,4,512]{3,2,1,0:T(4,128)(2,1)S(1)}, bf16[1,4,4,512]{3,2,1,0:T(4,128)(2,1)S(1)}, u32[]{:S(2)}, u32[]{:S(2)}) collective-permute-start(bf16[1,4,4,512]{3,2,1,0:T(4,128)(2,1)S(1)} %bitcast_select_fusion), channel_id=1, source_target_pairs={{0,1},{1,0},{2,3},{3,2},{4,5},{5,4},{6,7},{7,6},{8,9},{9,8},{10,11... | collective-permute-start | bytes 49160 | tf_op jit(solution)/shard_map/ppermute | solution.py:31
  19.6 4.0 %copy-start.1 = (s32[4]{0:T(128)S(1)}, s32[4]{0:T(128)}, u32[]{:S(2)}) copy-start(s32[4]{0:T(128)} %param.14) | copy-start | bytes 52
  23.7 10.3 %copy-start = (f32[4096]{0:T(1024)S(1)}, f32[4096]{0:T(1024)}, u32[]{:S(2)}) copy-start(f32[4096]{0:T(1024)} %param.9) | copy-start | bytes 49156
  23.9 4.0 %collective-permute-start.1 = (bf16[2,4,4,512]{3,2,1,0:T(4,128)(2,1)S(1)}, bf16[2,4,4,512]{3,2,1,0:T(4,128)(2,1)S(1)}, u32[]{:S(2)}, u32[]{:S(2)}) collective-permute-start(bf16[2,4,4,512]{3,2,1,0:T(4,128)(2,1)S(1)} %get-tuple-element.20), channel_id=1, source_target_pairs={{0,2},{1,3},{2,0},{3,1},{4,6},{5,7},{6,4},{7,5},{8,10},{9,11},{10,... | collective-permute-start | bytes 98312 | tf_op jit(solution)/shard_map/ppermute | solution.py:31
  28.0 5.2 %collective-permute-start.2 = (bf16[4,4,4,512]{3,2,1,0:T(4,128)(2,1)S(1)}, bf16[4,4,4,512]{3,2,1,0:T(4,128)(2,1)S(1)}, u32[]{:S(2)}, u32[]{:S(2)}) collective-permute-start(bf16[4,4,4,512]{3,2,1,0:T(4,128)(2,1)S(1)} %bitcast.133), channel_id=1, source_target_pairs={{0,4},{1,5},{2,6},{3,7},{4,0},{5,1},{6,2},{7,3},{8,12},{9,13},{10,... | collective-permute-start | bytes 196616 | tf_op jit(solution)/shard_map/ppermute | solution.py:31
  73.5 11.2 %all-to-all-start.1 = ((bf16[1,4,32,4]{3,1,0,2:T(4,128)(2,1)}), bf16[1,4,32,4]{3,1,0,2:T(4,128)(2,1)S(1)}, u32[]{:S(2)}, u32[]{:S(2)}) async-start(bf16[1,4,32,4]{3,1,0,2:T(4,128)(2,1)} %bitcast.26), calls=%async_computation.1 | async-start | bytes 65536 | tf_op jit(solution)/shard_map/all_to_all | solution.py:125
  84.7 10.0 %all-to-all-start.2 = ((bf16[1,4,32,4]{3,1,0,2:T(4,128)(2,1)}), bf16[1,4,32,4]{3,1,0,2:T(4,128)(2,1)S(1)}, u32[]{:S(2)}, u32[]{:S(2)}) async-start(bf16[1,4,32,4]{3,1,0,2:T(4,128)(2,1)} %bitcast.37), calls=%async_computation.2 | async-start | bytes 65536 | tf_op jit(solution)/shard_map/all_to_all | solution.py:118
  94.7 10.7 %all-to-all-start = ((bf16[1,4,32,4,128]{4,3,1,0,2:T(4,128)(2,1)}), bf16[1,4,32,4,128]{4,3,1,0,2:T(4,128)(2,1)S(1)}, u32[]{:S(2)}, u32[]{:S(2)}) async-start(bf16[1,4,32,4,128]{4,3,1,0,2:T(4,128)(2,1)} %copy.100), calls=%async_computation | async-start | bytes 262144 | tf_op jit(solution)/shard_map/all_to_all | solution.py:111
  98.1 84.2 %reduce-scatter.4.cloned.1.call-start = ((), (), s32[]{:S(2)}) async-start(), calls=%async_computation.4 | async-start | bytes 1179648
Sparse Core Ops, SparseCore 0:
  119.6 62.6 reduce-scatter.3
